TPU v7x, 32 devices: a whole 2x2x4 slice. The times are simulated.
32 devices in a mesh: ctx: 16 (over z, y, core), head: 2 (over x).
Axes of the slice: x: 2, y: 2, z: 4, core: 2. Of those that a mesh axis runs over, the one named last changes fastest.
Arguments:
- loader_query_rows: bfloat16 [6144, 8192], P(('ctx', 'head')), may hold values from -6 to 6
- loader_key_rows: bfloat16 [6144, 1024], P(('ctx', 'head')), may hold values from -6 to 6
- loader_value_rows: bfloat16 [6144, 1024], P(('ctx', 'head')), may hold values from -6 to 6
- output_gradient_rows: bfloat16 [6144, 8192], P(('ctx', 'head')), may hold values from -6 to 6
- doc_blocks: int32 [2, 3], replicated, may hold values from 1 to 16, as said below
- block_perm: int32 [48], replicated, may hold values from 0 to 47, as said below
Outputs:
- attn_out: bfloat16 [6144, 8192], P('ctx', 'head')
- grad_query: bfloat16 [6144, 8192], P('ctx', 'head')
- key_gradient: bfloat16 [6144, 1024], P('ctx', 'head')
- value_gradient: bfloat16 [6144, 1024], P('ctx', 'head')
Inputs may be any that keep to these rules, and one draw needn't show every extreme that they name: doc_blocks[g] lists in order the lengths, in blocks, of the documents that fill row blocks g * 24 to (g + 1) * 24 - 1 of the packed row; each row sums to 24 and holds one length equal to 16. block_perm is a permutation that maps the blocks of each aligned span of 24 blocks onto the same span.
All inputs are finite; a program needn't handle non-finite values.
Results may differ from a plain program's by a relative error of at most 0.012.
The roundings to bfloat16 on the way count: a program that leaves them out, or rounds other values in their place, can miss the bound.
Values may be sent and summed in bfloat16 or wider, within the bound.
A program may use at most 192 MiB of HBM per device.

v0:
```python
from functools import partial
import math

import jax
import jax.numpy as jnp
from jax import lax
from jax.experimental import pallas as pl
from jax.experimental.pallas import tpu as pltpu
from jax.sharding import PartitionSpec as P

QUERY_HEADS = 64
KEY_VALUE_HEADS = 8
HEAD_SIZE = 128
MASK_BLOCK_SIZE = 128
GROUP_DEV = 8
GROUP_BLOCKS = 24
MOST = 16

RATIO = QUERY_HEADS // KEY_VALUE_HEADS
MASKED_LOGIT = -1e30
CHUNK = 512
SPAN_TOKENS = GROUP_BLOCKS * MASK_BLOCK_SIZE
MESH = pl.DeviceIdType.MESH


def doc_first(doc_blocks):
    ends = jnp.cumsum(doc_blocks)
    firsts = ends - doc_blocks
    blocks = jnp.arange(GROUP_BLOCKS, dtype=jnp.int32)
    return jnp.max(jnp.where(firsts[None, :] <= blocks[:, None], firsts[None, :], 0), axis=1)


def enter(peers):
    barrier = pltpu.get_barrier_semaphore()
    for peer in peers:
        pl.semaphore_signal(barrier, inc=1, device_id=peer, device_id_type=MESH)
    pl.semaphore_wait(barrier, len(peers))


def flipped(index, mask, count):
    result, bit = index, 1
    while bit < count:
        if mask & bit:
            result = result + bit - index // bit % 2 * (2 * bit)
        bit *= 2
    return result


def visiting_order(members):
    return SPREAD_ORDER if len(SPREAD_ORDER) == members - 1 else list(range(members - 1, 0, -1))


SPREAD_ORDER = [13, 5, 9, 15, 7, 11, 12, 4, 8, 14, 6, 10, 1, 3, 2]


def spread_kernel(head_dim, query_ref, grad_ref, pair_ref, *rest):
    query_out, grad_out, pair_out, query_stage, grad_stage, pair_stage = rest[:6]
    send_sems, recv_sems, pass_send_sems, pass_recv_sems, local_sems = rest[6:]
    members = GROUP_DEV * head_dim
    rows = query_ref.shape[0]
    wide = query_out.shape[1]
    heads = wide // HEAD_SIZE
    ctx = lax.axis_index("ctx")
    head = lax.axis_index("head")
    base = ctx // GROUP_DEV * GROUP_DEV
    lane = ctx - base
    own = lane * head_dim + head
    order = visiting_order(members)

    def columns(peer_lane, peer_head):
        worker = peer_head * GROUP_DEV + peer_lane
        query_at = pl.ds(pl.multiple_of(worker * wide, HEAD_SIZE), wide)
        key_at = pl.ds(
            pl.multiple_of(worker * heads // RATIO * HEAD_SIZE, HEAD_SIZE), HEAD_SIZE
        )
        return query_at, key_at

    def rows_of(member):
        return pl.ds(pl.multiple_of(member * rows, 16), rows)

    landing = rows_of(own)
    kind = lane % 2
    query_at, key_at = columns(lane, head)
    loads = [
        pltpu.make_async_copy(pair_ref.at[kind, :, key_at], pair_stage, local_sems.at[0]),
        pltpu.make_async_copy(query_ref.at[:, query_at], query_stage, local_sems.at[1]),
        pltpu.make_async_copy(grad_ref.at[:, query_at], grad_stage, local_sems.at[2]),
    ]
    for load in loads:
        load.start()
    peers = []
    for mask in order:
        member = flipped(own, mask, members)
        peers.append((member, member // head_dim, member % head_dim))
    device = [{"ctx": base + peer_lane, "head": peer_head} for _, peer_lane, peer_head in peers]
    sibling = {"ctx": base + flipped(lane, 1, GROUP_DEV), "head": head}
    enter(device)
    pair_copies, copies = [], []
    for step, (member, peer_lane, peer_head) in enumerate(peers):
        key_at = columns(peer_lane, peer_head)[1]
        copy = pltpu.make_async_remote_copy(
            src_ref=pair_ref.at[peer_lane % 2, :, key_at],
            dst_ref=pair_out.at[peer_lane % 2, landing, :],
            send_sem=send_sems.at[2, step],
            recv_sem=recv_sems.at[2, step],
            device_id=device[step],
            device_id_type=MESH,
        )
        copy.start()
        pair_copies.append(copy)
    for step, (member, peer_lane, peer_head) in enumerate(peers):
        query_at = columns(peer_lane, peer_head)[0]
        for index, (source, target) in enumerate(
            ((query_ref, query_out), (grad_ref, grad_out))
        ):
            copy = pltpu.make_async_remote_copy(
                src_ref=source.at[:, query_at],
                dst_ref=target.at[landing, :],
                send_sem=send_sems.at[index, step],
                recv_sem=recv_sems.at[index, step],
                device_id=device[step],
                device_id_type=MESH,
            )
            copy.start()
            copies.append(copy)
    stores = []
    for index, (stage, target) in enumerate(
        (
            (pair_stage, pair_out.at[kind, landing, :]),
            (query_stage, query_out.at[landing, :]),
            (grad_stage, grad_out.at[landing, :]),
        )
    ):
        loads[index].wait()
        store = pltpu.make_async_copy(stage, target, local_sems.at[3 + index])
        store.start()
        stores.append(store)

    def passing(slot, source, spot):
        copy = pltpu.make_async_remote_copy(
            src_ref=source,
            dst_ref=pair_out.at[kind, spot, :],
            send_sem=pass_send_sems.at[slot],
            recv_sem=pass_recv_sems.at[slot],
            device_id=sibling,
            device_id_type=MESH,
        )
        copy.start()
        return copy

    passes = [passing(members - 1, pair_stage, landing)]
    for step, (member, peer_lane, peer_head) in enumerate(peers):
        pair_copies[step].wait_recv()
        spot = rows_of(member)
        passes.append(passing(step, pair_out.at[kind, spot, :], spot))
    for store in stores:
        store.wait()
    for copy in pair_copies:
        copy.wait_send()
    for copy in copies:
        copy.wait()
    for copy in passes:
        copy.wait()


def spread(head_dim, query, grad, pair):
    rows, width = query.shape
    members = GROUP_DEV * head_dim
    wide = width // members
    any_spec = pl.BlockSpec(memory_space=pl.ANY)
    return pl.pallas_call(
        partial(spread_kernel, head_dim),
        out_shape=[
            jax.ShapeDtypeStruct((rows * members, wide), jnp.bfloat16),
            jax.ShapeDtypeStruct((rows * members, wide), jnp.bfloat16),
            jax.ShapeDtypeStruct((2, rows * members, HEAD_SIZE), jnp.bfloat16),
        ],
        in_specs=[any_spec] * 3,
        out_specs=[any_spec] * 3,
        scratch_shapes=[
            pltpu.VMEM((rows, wide), jnp.bfloat16),
            pltpu.VMEM((rows, wide), jnp.bfloat16),
            pltpu.VMEM((rows, HEAD_SIZE), jnp.bfloat16),
            pltpu.SemaphoreType.DMA((3, members - 1)),
            pltpu.SemaphoreType.DMA((3, members - 1)),
            pltpu.SemaphoreType.DMA((members,)),
            pltpu.SemaphoreType.DMA((members,)),
            pltpu.SemaphoreType.DMA((6,)),
        ],
        compiler_params=pltpu.CompilerParams(collective_id=0, has_side_effects=True),
        name="spread",
    )(query, grad, pair)


def gather_kernel(attn_ref, query_ref, pair_ref, *rest):
    attn_out, query_out, pair_out, attn_stage, query_stage, mine, other = rest[:7]
    send_sems, recv_sems, swap_sems, local_sems = rest[7:]
    rows = attn_out.shape[0]
    wide = attn_ref.shape[1]
    sharers = RATIO // (wide // HEAD_SIZE)
    ctx = lax.axis_index("ctx")
    head = lax.axis_index("head")
    base = ctx // GROUP_DEV * GROUP_DEV
    lane = ctx - base
    kind = lane % 2
    own_at = pl.ds(pl.multiple_of(lane * wide, HEAD_SIZE), wide)
    pair_at = pl.ds(pl.multiple_of(lane // sharers * HEAD_SIZE, HEAD_SIZE), HEAD_SIZE)
    pair_landing = pair_out.at[kind, lane % sharers // 2, :, pair_at]

    def taken(peer):
        return pl.ds(pl.multiple_of(peer * rows, 16), rows)

    loads = [
        pltpu.make_async_copy(pair_ref.at[kind], mine, local_sems.at[0]),
        pltpu.make_async_copy(attn_ref.at[taken(lane), :], attn_stage, local_sems.at[1]),
        pltpu.make_async_copy(query_ref.at[taken(lane), :], query_stage, local_sems.at[2]),
    ]
    for load in loads:
        load.start()
    peers = [flipped(lane, mask, GROUP_DEV) for mask in GATHER_ORDER]
    device = [{"ctx": base + peer, "head": head} for peer in peers]
    enter(device)
    swap = pltpu.make_async_remote_copy(
        src_ref=pair_ref.at[1 - kind],
        dst_ref=other,
        send_sem=swap_sems.at[0],
        recv_sem=swap_sems.at[1],
        device_id={"ctx": base + flipped(lane, 1, GROUP_DEV), "head": head},
        device_id_type=MESH,
    )
    swap.start()
    copies = []
    for step, peer in enumerate(peers):
        for index, (source, target) in enumerate(((attn_ref, attn_out), (query_ref, query_out))):
            copy = pltpu.make_async_remote_copy(
                src_ref=source.at[taken(peer), :],
                dst_ref=target.at[:, own_at],
                send_sem=send_sems.at[index, step],
                recv_sem=recv_sems.at[index, step],
                device_id=device[step],
                device_id_type=MESH,
            )
            copy.start()
            copies.append(copy)
    stores = []
    for index, (stage, target) in ((1, (attn_stage, attn_out)), (2, (query_stage, query_out))):
        loads[index].wait()
        store = pltpu.make_async_copy(stage, target.at[:, own_at], local_sems.at[2 + index])
        store.start()
        stores.append(store)
    loads[0].wait()
    swap.wait()
    for peer in range(GROUP_DEV):
        at = slice(peer * rows, (peer + 1) * rows)
        total = mine[at, :].astype(jnp.float32) + other[at, :].astype(jnp.float32)
        mine[at, :] = total.astype(jnp.bfloat16)
    store = pltpu.make_async_copy(mine.at[taken(lane), :], pair_landing, local_sems.at[5])
    store.start()
    stores.append(store)
    for step, peer in enumerate(peers):
        copy = pltpu.make_async_remote_copy(
            src_ref=mine.at[taken(peer), :],
            dst_ref=pair_landing,
            send_sem=send_sems.at[2, step],
            recv_sem=recv_sems.at[2, step],
            device_id=device[step],
            device_id_type=MESH,
        )
        copy.start()
        copies.append(copy)
    for store in stores:
        store.wait()
    for copy in copies:
        copy.wait()


GATHER_ORDER = [6, 2, 4, 7, 3, 5, 1]


def gather(attn, query, pair):
    tokens, wide = attn.shape
    rows = tokens // GROUP_DEV
    sharers = RATIO // (wide // HEAD_SIZE)
    any_spec = pl.BlockSpec(memory_space=pl.ANY)
    return pl.pallas_call(
        gather_kernel,
        out_shape=[
            jax.ShapeDtypeStruct((rows, wide * GROUP_DEV), jnp.bfloat16),
            jax.ShapeDtypeStruct((rows, wide * GROUP_DEV), jnp.bfloat16),
            jax.ShapeDtypeStruct(
                (2, sharers // 2, rows, HEAD_SIZE * GROUP_DEV // sharers), jnp.bfloat16
            ),
        ],
        in_specs=[any_spec] * 3,
        out_specs=[any_spec] * 3,
        scratch_shapes=[
            pltpu.VMEM((rows, wide), jnp.bfloat16),
            pltpu.VMEM((rows, wide), jnp.bfloat16),
            pltpu.VMEM((tokens, HEAD_SIZE), jnp.bfloat16),
            pltpu.VMEM((tokens, HEAD_SIZE), jnp.bfloat16),
            pltpu.SemaphoreType.DMA((3, GROUP_DEV - 1)),
            pltpu.SemaphoreType.DMA((3, GROUP_DEV - 1)),
            pltpu.SemaphoreType.DMA((2,)),
            pltpu.SemaphoreType.DMA((6,)),
        ],
        compiler_params=pltpu.CompilerParams(collective_id=1, has_side_effects=True),
        name="gather",
    )(attn, query, pair)


def dot(left, right):
    return jnp.dot(left, right, preferred_element_type=jnp.float32)


def attend_kernel(
    firsts_ref,
    places_ref,
    query_ref,
    grad_ref,
    pair_ref,
    attn_ref,
    query_grad_ref,
    pair_grad_ref,
    keys,
    values,
    keys_t,
    values_t,
    store,
    out_t,
    query_grad_t,
    key_total,
    value_total,
):
    heads = query_ref.shape[1] // HEAD_SIZE
    block = MASK_BLOCK_SIZE
    columns = heads * block
    half = SPAN_TOKENS // 2
    scale = HEAD_SIZE ** (-0.5)
    scale_log2 = scale * math.log2(math.e)
    tail = keys.shape[0] - SPAN_TOKENS
    for kind, flat, turned in ((0, keys, keys_t), (1, values, values_t)):
        flat[0:half, :] = pair_ref[kind, half:SPAN_TOKENS, :]
        flat[half:SPAN_TOKENS, :] = pair_ref[kind, 0:half, :]
        flat[SPAN_TOKENS:, :] = jnp.zeros((tail, HEAD_SIZE), jnp.bfloat16)
        turned[:, SPAN_TOKENS:] = jnp.zeros((HEAD_SIZE, tail), jnp.bfloat16)
    for index in range(GROUP_BLOCKS):
        at = slice(index * block, (index + 1) * block)
        keys_t[:, at] = keys[at, :].T
        values_t[:, at] = values[at, :].T
    key_total[...] = jnp.zeros_like(key_total)
    value_total[...] = jnp.zeros_like(value_total)
    token = lax.rem(lax.broadcasted_iota(jnp.int32, (CHUNK, columns), 1), block)
    key_at = lax.broadcasted_iota(jnp.int32, (CHUNK, columns), 0)
    ahead = key_at - token

    def one_block(index, _):
        first = firsts_ref[index]
        count = index - first + 1
        steps = (count * block + CHUNK - 1) // CHUNK
        loader = lax.rem(index + GROUP_BLOCKS // 2, GROUP_BLOCKS)
        source = pl.ds(pl.multiple_of(loader * block, block), block)
        target = pl.ds(pl.multiple_of(places_ref[loader] * block, block), block)
        parts = [slice(h * HEAD_SIZE, (h + 1) * HEAD_SIZE) for h in range(heads)]
        query = jnp.concatenate([query_ref[source, at] for at in parts], axis=0)
        grad = jnp.concatenate([grad_ref[source, at] for at in parts], axis=0)
        query_t = jnp.concatenate([query_ref[source, at].T for at in parts], axis=1)
        grad_t = jnp.concatenate([grad_ref[source, at].T for at in parts], axis=1)

        def spot(step):
            return pl.ds(pl.multiple_of(first * block + step * CHUNK, block), CHUNK)

        def slot(step):
            return pl.ds(pl.multiple_of(step * CHUNK, CHUNK), CHUNK)

        def logits(step, peak):
            raw = dot(keys[spot(step), :], query_t)
            bound = (count - 1) * block - step * CHUNK
            raw = jnp.where(ahead <= bound, raw, MASKED_LOGIT)
            store[slot(step), :] = raw
            return jnp.maximum(peak, jnp.max(raw, axis=0, keepdims=True))

        peak = lax.fori_loop(
            0, steps, logits, jnp.full((1, columns), MASKED_LOGIT, jnp.float32)
        )
        peak = peak * scale_log2
        out_t[...] = jnp.zeros_like(out_t)

        def mix(step, total):
            mass = jnp.exp2(store[slot(step), :] * scale_log2 - peak)
            store[slot(step), :] = mass
            out_t[...] += dot(values_t[:, spot(step)], mass.astype(jnp.bfloat16))
            return total + jnp.sum(mass, axis=0, keepdims=True)

        total = lax.fori_loop(0, steps, mix, jnp.zeros((1, columns), jnp.float32))
        share = 1.0 / total
        out = (out_t[...] * share).astype(jnp.bfloat16)
        delta = jnp.sum(
            out.astype(jnp.float32) * grad_t.astype(jnp.float32), axis=0, keepdims=True
        )
        for h, at in enumerate(parts):
            attn_ref[target, at] = out[:, h * block : (h + 1) * block].T
        query_grad_t[...] = jnp.zeros_like(query_grad_t)

        def back(step, carry):
            weights = store[slot(step), :] * share
            value_total[spot(step), :] += dot(weights.astype(jnp.bfloat16), grad)
            grad_weights = dot(values[spot(step), :], grad_t)
            dlogits = (weights * (grad_weights - delta)).astype(jnp.bfloat16)
            key_total[spot(step), :] += dot(dlogits, query)
            query_grad_t[...] += dot(keys_t[:, spot(step)], dlogits)
            return carry

        lax.fori_loop(0, steps, back, 0)
        moved = (query_grad_t[...] * scale).astype(jnp.bfloat16)
        for h, at in enumerate(parts):
            query_grad_ref[target, at] = moved[:, h * block : (h + 1) * block].T
        return 0

    lax.fori_loop(0, GROUP_BLOCKS, one_block, 0)

    def finish(index, _):
        loader = lax.rem(index + GROUP_BLOCKS // 2, GROUP_BLOCKS)
        source = pl.ds(pl.multiple_of(index * block, block), block)
        target = pl.ds(pl.multiple_of(places_ref[loader] * block, block), block)
        pair_grad_ref[0, target, :] = (key_total[source, :] * scale).astype(jnp.bfloat16)
        pair_grad_ref[1, target, :] = value_total[source, :].astype(jnp.bfloat16)
        return 0

    lax.fori_loop(0, GROUP_BLOCKS, finish, 0)


def attend(firsts, places, query, grad, pair):
    wide = query.shape[1]
    columns = wide // HEAD_SIZE * MASK_BLOCK_SIZE
    padded = SPAN_TOKENS + CHUNK - MASK_BLOCK_SIZE
    vmem = pl.BlockSpec(memory_space=pltpu.VMEM)
    smem = pl.BlockSpec(memory_space=pltpu.SMEM)
    return pl.pallas_call(
        attend_kernel,
        out_shape=[
            jax.ShapeDtypeStruct(query.shape, jnp.bfloat16),
            jax.ShapeDtypeStruct(query.shape, jnp.bfloat16),
            jax.ShapeDtypeStruct(pair.shape, jnp.bfloat16),
        ],
        in_specs=[smem, smem, vmem, vmem, vmem],
        out_specs=[vmem] * 3,
        scratch_shapes=[
            pltpu.VMEM((padded, HEAD_SIZE), jnp.bfloat16),
            pltpu.VMEM((padded, HEAD_SIZE), jnp.bfloat16),
            pltpu.VMEM((HEAD_SIZE, padded), jnp.bfloat16),
            pltpu.VMEM((HEAD_SIZE, padded), jnp.bfloat16),
            pltpu.VMEM((MOST * MASK_BLOCK_SIZE, columns), jnp.float32),
            pltpu.VMEM((HEAD_SIZE, columns), jnp.float32),
            pltpu.VMEM((HEAD_SIZE, columns), jnp.float32),
            pltpu.VMEM((padded, HEAD_SIZE), jnp.float32),
            pltpu.VMEM((padded, HEAD_SIZE), jnp.float32),
        ],
        compiler_params=pltpu.CompilerParams(vmem_limit_bytes=60 * 1024 * 1024),
        name="attend",
    )(firsts, places, query, grad, pair)


def body(head_dim, query_rows, key_rows, value_rows, grad_rows, doc_blocks, block_perm):
    group = lax.axis_index("ctx") // GROUP_DEV
    firsts = doc_first(lax.dynamic_index_in_dim(doc_blocks, group, 0, keepdims=False))
    places = lax.dynamic_slice_in_dim(block_perm, group * GROUP_BLOCKS, GROUP_BLOCKS)
    places = places - group * GROUP_BLOCKS
    query, grad, pair = spread(head_dim, query_rows, grad_rows, jnp.stack([key_rows, value_rows]))
    attn, query_grad, parts = gather(*attend(firsts, places, query, grad, pair))
    if parts.shape[1] > 1:
        parts = jnp.sum(parts.astype(jnp.float32), axis=1).astype(jnp.bfloat16)
    else:
        parts = parts[:, 0]
    return attn, query_grad, parts[0], parts[1]


def solution(mesh):
    split = P(("ctx", "head"), None)
    out_spec = P("ctx", "head")
    return jax.shard_map(
        partial(body, mesh.shape["head"]),
        mesh=mesh,
        in_specs=(split, split, split, split, P(), P()),
        out_specs=(out_spec,) * 4,
        check_vma=False,
    )
```

profile of v0, /device:TPU:0, one launch (start us, length us, event | category | flops | bytes accessed | tf_op | source)
XLA Modules:
  0.0 266.1 jit_solution(17049834914718690996)
XLA Ops:
  0.7 1.2 dynamic-slice_subtract_fusion.places_ref
  1.9 0.7 constant_dynamic-slice_fusion
  2.6 0.2 reduce-window_clone.1
  2.8 0.7 subtract_bitcast_fusion
  3.4 0.6 select_reduce_fusion.firsts_ref
  4.0 2.1 pad_maximum_fusion.pair_ref
  6.1 92.4 %spread.1 = (bf16[3072,512]{1,0:T(8,128)(2,1)}, bf16[3072,512]{1,0:T(8,128)(2,1)}, bf16[2,3072,128]{2,1,0:T(8,128)(2,1)}) custom-call(bf16[192,8192]{1,0:T(8,128)(2,1)} %query_ref.1, bf16[192,8192]{1,0:T(8,128)(2,1)} %grad_ref.1, bf16[2,192,1024]{2,1,0:T(8,128)(2,1)} %pad_maximum_fusion.pair_ref), custom_call_target="tpu_custom_call" | custom-call | tf_op jit(solution)/shard_map/spread/pallas_call | solution.py:171
  98.5 80.4 %attend.1 = (bf16[3072,512]{1,0:T(8,128)(2,1)}, bf16[3072,512]{1,0:T(8,128)(2,1)}, bf16[2,3072,128]{2,1,0:T(8,128)(2,1)}) custom-call(s32[24]{0:T(128)} %select_reduce_fusion.firsts_ref, s32[24]{0:T(128)} %dynamic-slice_subtract_fusion.places_ref, bf16[3072,512]{1,0:T(8,128)(2,1)} %get-tuple-element.13.query_ref, ...), custom_call_target="tpu_custom_call" | custom-call | tf_op jit(solution)/shard_map/attend/pallas_call | solution.py:438
  179.0 79.3 %gather.1 = (bf16[384,4096]{1,0:T(8,128)(2,1)}, bf16[384,4096]{1,0:T(8,128)(2,1)}, bf16[2,1,384,512]{3,2,1,0:T(8,128)(2,1)}) custom-call(bf16[3072,512]{1,0:T(8,128)(2,1)} %get-tuple-element.16.attn_ref, bf16[3072,512]{1,0:T(8,128)(2,1)} %get-tuple-element.17.query_ref, bf16[2,3072,128]{2,1,0:T(8,128)(2,1)} %get-tuple-element.18.pair_ref), custom_call_target="tpu_custom_call" | custom-call | tf_op jit(solution)/shard_map/gather/pallas_call | solution.py:285
  258.3 2.0 slice_bitcast_fusion
  260.4 0.0 copy-start
  260.4 4.1 %copy.12 = bf16[384,4096]{1,0:T(8,128)(2,1)} copy(bf16[384,4096]{1,0:T(8,128)(2,1)} %get-tuple-element.28) | data formatting | bytes 6291456
  264.4 0.0 copy-done
  264.4 1.7 copy.13
Async XLA Ops:
  260.4 4.1 %copy-start = (bf16[384,4096]{1,0:T(8,128)(2,1)S(1)}, bf16[384,4096]{1,0:T(8,128)(2,1)}, u32[]{:S(2)}) copy-start(bf16[384,4096]{1,0:T(8,128)(2,1)} %get-tuple-element.29) | copy-start | bytes 9437188
where the time goes:
time: 267 us; the launch traced here: 266 us
  Pallas kernels  252 us (94%)
  local copies, waits for them, and re-layouts  8.45 us (3%)
  other arithmetic  4.77 us (2%)
    pallas_call x1, Pallas kernels, spread(): pl.pallas_call(partial(spread_kernel, head_dim), out_shape=[jax.ShapeDtyp...  92.4 us
    pallas_call x1, Pallas kernels, attend(): pl.pallas_call(attend_kernel, out_shape=[jax.ShapeDtypeStruct(query.shape...  80.4 us
    pallas_call x1, Pallas kernels, gather(): pl.pallas_call(gather_kernel, out_shape=[jax.ShapeDtypeStruct((rows, wide...  79.3 us
    unnamed x4, local copies, waits for them, and re-layouts  5.72 us

commit v1 on v0

v1 whole, which is shorter than its diff:
```python
from functools import partial
import math

import jax
import jax.numpy as jnp
from jax import lax
from jax.experimental import pallas as pl
from jax.experimental.pallas import tpu as pltpu
from jax.sharding import PartitionSpec as P

QUERY_HEADS = 64
KEY_VALUE_HEADS = 8
HEAD_SIZE = 128
MASK_BLOCK_SIZE = 128
GROUP_DEV = 8
GROUP_BLOCKS = 24
MOST = 16

RATIO = QUERY_HEADS // KEY_VALUE_HEADS
MASKED_LOGIT = -1e30
CHUNK = 512
SPAN_TOKENS = GROUP_BLOCKS * MASK_BLOCK_SIZE
LONG_TOKENS = MOST * MASK_BLOCK_SIZE
MESH = pl.DeviceIdType.MESH

SPREAD_ORDER = [13, 5, 9, 15, 7, 11, 12, 4, 8, 14, 6, 10, 1, 3, 2]
GATHER_ORDER = [6, 2, 4, 7, 3, 5, 1]


def enter(peers):
    barrier = pltpu.get_barrier_semaphore()
    for peer in peers:
        pl.semaphore_signal(barrier, inc=1, device_id=peer, device_id_type=MESH)
    pl.semaphore_wait(barrier, len(peers))


def flipped(index, mask, count):
    result, bit = index, 1
    while bit < count:
        if mask & bit:
            result = result + bit - index // bit % 2 * (2 * bit)
        bit *= 2
    return result


def visiting_order(members):
    return SPREAD_ORDER if len(SPREAD_ORDER) == members - 1 else list(range(members - 1, 0, -1))


def dot(left, right):
    return jnp.dot(left, right, preferred_element_type=jnp.float32)


def copy_to(source, target, send_sem, recv_sem, device):
    return pltpu.make_async_remote_copy(
        src_ref=source,
        dst_ref=target,
        send_sem=send_sem,
        recv_sem=recv_sem,
        device_id=device,
        device_id_type=MESH,
    )


def fused_kernel(head_dim, heads, *refs):
    refs = list(refs)

    def take(count):
        taken, refs[:] = refs[:count], refs[count:]
        return taken

    docs_ref, perm_ref, query_ref, grad_ref, key_ref, value_ref = take(6)
    attn_out, query_grad_out, pair_out = take(3)
    query_land, grad_land = take(heads), take(heads)
    (pair_land,) = take(1)
    query_s, grad_s, query_t, grad_t, keys, values, keys_t, values_t = take(8)
    store, out_t, query_grad_t, key_total, value_total, out_s, query_grad_s = take(7)
    attn_place, query_grad_place, pair_place, other, mine = take(5)
    slot_at, source_at, place_at = take(3)
    in_send, in_recv, pair_send, pair_recv, pass_send, pass_recv = take(6)
    out_send, out_recv, part_send, part_recv, swap_sems, local_sems, out_local = take(7)

    members = GROUP_DEV * head_dim
    units, unit, _ = query_ref.shape
    wide = heads * HEAD_SIZE
    block = MASK_BLOCK_SIZE
    per_block = block // unit
    per_chunk = CHUNK // block
    out_rows = SPAN_TOKENS // GROUP_DEV
    sharers = RATIO // heads
    scale = HEAD_SIZE ** (-0.5)
    scale_log2 = scale * math.log2(math.e)

    ctx = lax.axis_index("ctx")
    head = lax.axis_index("head")
    group = ctx // GROUP_DEV
    base = group * GROUP_DEV
    lane = ctx - base
    kind = lane % 2
    own = lane * head_dim + head
    order = visiting_order(members)

    def rows_of(member):
        return pl.ds(member * units, units)

    def head_columns(peer_lane, peer_head, h):
        worker = peer_head * GROUP_DEV + peer_lane
        return pl.ds(pl.multiple_of(worker * wide + h * HEAD_SIZE, HEAD_SIZE), HEAD_SIZE)

    def key_columns(peer_lane, peer_head):
        worker = peer_head * GROUP_DEV + peer_lane
        return pl.ds(
            pl.multiple_of(worker * heads // RATIO * HEAD_SIZE, HEAD_SIZE), HEAD_SIZE
        )

    landing = rows_of(own)
    masks = [(mask, flipped(own, mask, members)) for mask in order]
    peers = [(mask, member, member // head_dim, member % head_dim) for mask, member in masks]
    device = [{"ctx": base + peer_lane, "head": peer_head} for _, _, peer_lane, peer_head in peers]
    sibling = {"ctx": base + flipped(lane, 1, GROUP_DEV), "head": head}

    def own_pair(own_kind):
        return pltpu.make_async_copy(
            (key_ref, value_ref)[own_kind].at[:, :, key_columns(lane, head)],
            pair_land.at[own_kind, landing],
            local_sems.at[2 * heads],
        )

    def pair_copy(step, peer_kind):
        _, _, peer_lane, peer_head = peers[step]
        return copy_to(
            (key_ref, value_ref)[peer_kind].at[:, :, key_columns(peer_lane, peer_head)],
            pair_land.at[peer_kind, landing],
            pair_send.at[step],
            pair_recv.at[step],
            device[step],
        )

    loads = []
    for h in range(heads):
        at = head_columns(lane, head, h)
        for index, (source, target) in enumerate(
            ((query_ref, query_land[h]), (grad_ref, grad_land[h]))
        ):
            load = pltpu.make_async_copy(
                source.at[:, :, at], target.at[landing], local_sems.at[2 * h + index]
            )
            load.start()
            loads.append(load)
    for own_kind in range(2):

        @pl.when(kind == own_kind)
        def _(own_kind=own_kind):
            own_pair(own_kind).start()

    enter(device)
    for own_kind in range(2):

        @pl.when(kind == own_kind)
        def _(own_kind=own_kind):
            for step, (mask, _, _, _) in enumerate(peers):
                pair_copy(step, (own_kind + mask // head_dim) % 2).start()

    head_copies = []
    for h in range(heads):
        copies = []
        for step, (_, _, peer_lane, peer_head) in enumerate(peers):
            at = head_columns(peer_lane, peer_head, h)
            for index, (source, target) in enumerate(
                ((query_ref, query_land[h]), (grad_ref, grad_land[h]))
            ):
                copy = copy_to(
                    source.at[:, :, at],
                    target.at[landing],
                    in_send.at[h, index, step],
                    in_recv.at[h, index, step],
                    device[step],
                )
                copy.start()
                copies.append(copy)
        head_copies.append(copies)

    lengths = [docs_ref[group, i] for i in range(docs_ref.shape[1])]
    starts, start = [], jnp.int32(0)
    for length in lengths:
        starts.append(start)
        start = start + length
    big = jnp.int32(0)
    for length, start in zip(lengths, starts):
        big = big + jnp.where(length == MOST, start, 0)
    other_starts = [
        jnp.where(length == MOST, 0, start - jnp.where(start > big, MOST, 0)) * block
        for length, start in zip(lengths, starts)
    ]

    def loader_of(row_block):
        moved = row_block + GROUP_BLOCKS // 2
        return jnp.where(moved >= GROUP_BLOCKS, moved - GROUP_BLOCKS, moved)

    for slot in range(GROUP_BLOCKS):
        if slot < MOST:
            row_block = big + slot
        else:
            other_block = slot - MOST
            row_block = jnp.where(big <= other_block, slot, other_block)
        source_at[slot] = loader_of(row_block)
    for loader in range(GROUP_BLOCKS):
        row_block = (loader + GROUP_BLOCKS // 2) % GROUP_BLOCKS
        slot = row_block - big
        slot = jnp.where(slot >= MOST, row_block, slot)
        slot_at[loader] = jnp.where(slot < 0, row_block + MOST, slot)

    def find(place, _):
        found = jnp.int32(0)
        for loader in range(GROUP_BLOCKS):
            hit = perm_ref[group * GROUP_BLOCKS + loader] == group * GROUP_BLOCKS + place
            found = jnp.where(hit, slot_at[loader], found)
        place_at[place] = found
        return 0

    lax.fori_loop(0, GROUP_BLOCKS, find, 0)

    key_total[...] = jnp.zeros_like(key_total)
    value_total[...] = jnp.zeros_like(value_total)

    def passing(slot, spot):
        copy = copy_to(
            pair_land.at[kind, spot],
            pair_land.at[kind, spot],
            pass_send.at[slot],
            pass_recv.at[slot],
            sibling,
        )
        copy.start()
        return copy

    pltpu.make_async_copy(
        key_ref.at[:, :, key_columns(lane, head)],
        pair_land.at[kind, landing],
        local_sems.at[2 * heads],
    ).wait()
    passes = [passing(members - 1, landing)]
    pairs = []
    for step, (_, member, _, _) in enumerate(peers):
        pair = copy_to(
            key_ref.at[:, :, key_columns(lane, head)],
            pair_land.at[kind, rows_of(member)],
            pair_send.at[step],
            pair_recv.at[step],
            device[step],
        )
        pair.wait_recv()
        pairs.append(pair)
        passes.append(passing(step, rows_of(member)))
    for copy in passes:
        copy.wait()

    def to_slot(slot):
        return pl.ds(pl.multiple_of(slot * block, block), block)

    def take_pair(slot, _):
        source, target = source_at[slot] * per_block, to_slot(slot)
        for which, flat, turned in ((0, keys, keys_t), (1, values, values_t)):
            rows_in = [pair_land[which, source + part] for part in range(per_block)]
            rows_in = jnp.concatenate(rows_in, axis=0)
            flat[target, :] = rows_in
            turned[:, target] = rows_in.T
        return 0

    lax.fori_loop(0, GROUP_BLOCKS, take_pair, 0)

    token = lax.broadcasted_iota(jnp.int32, (CHUNK, CHUNK), 1)
    key_at = lax.broadcasted_iota(jnp.int32, (CHUNK, CHUNK), 0)

    def tile(first, index, short):
        at = pl.ds(pl.multiple_of(first + index * CHUNK, CHUNK), CHUNK)
        steps = index + 1

        def spot(step):
            return pl.ds(pl.multiple_of(first + step * CHUNK, CHUNK), CHUNK)

        def slot(step):
            return pl.ds(pl.multiple_of(step * CHUNK, CHUNK), CHUNK)

        def blocks(step):
            return pl.ds(first // block + step * per_chunk, per_chunk)

        def blocked(array):
            return array.reshape(per_chunk, block, HEAD_SIZE)

        queries_t = query_t[:, at]
        grads_t = grad_t[:, at]
        column = index * CHUNK + lax.broadcasted_iota(jnp.int32, (1, CHUNK), 1)
        opened = jnp.zeros((1, CHUNK), jnp.int32)
        if short:
            for start in other_starts:
                opened = jnp.maximum(opened, jnp.where(column >= start, start, 0))

        def logits(step, peak, diagonal):
            raw = dot(keys[spot(step), :], queries_t)
            if diagonal:
                allowed = key_at <= token
                if short:
                    allowed = allowed & (key_at >= opened - step * CHUNK)
                raw = jnp.where(allowed, raw, MASKED_LOGIT)
            elif short:
                raw = jnp.where(key_at >= opened - step * CHUNK, raw, MASKED_LOGIT)
            store[slot(step), :] = raw
            return jnp.maximum(peak, jnp.max(raw, axis=0, keepdims=True))

        peak = lax.fori_loop(
            0,
            index,
            lambda step, peak: logits(step, peak, False),
            jnp.full((1, CHUNK), MASKED_LOGIT, jnp.float32),
        )
        peak = logits(index, peak, True) * scale_log2
        out_t[...] = jnp.zeros_like(out_t)

        def mix(step, total):
            mass = jnp.exp2(store[slot(step), :] * scale_log2 - peak)
            store[slot(step), :] = mass
            out_t[...] += dot(values_t[:, spot(step)], mass.astype(jnp.bfloat16))
            return total + jnp.sum(mass, axis=0, keepdims=True)

        total = lax.fori_loop(0, steps, mix, jnp.zeros((1, CHUNK), jnp.float32))
        share = 1.0 / total
        out = (out_t[...] * share).astype(jnp.bfloat16)
        delta = jnp.sum(
            out.astype(jnp.float32) * grads_t.astype(jnp.float32), axis=0, keepdims=True
        )
        out_s[blocks(index)] = blocked(out.T)
        query_grad_t[...] = jnp.zeros_like(query_grad_t)

        def back(step, carry):
            weights = store[slot(step), :] * share
            value_total[blocks(step)] += blocked(dot(weights.astype(jnp.bfloat16), grad_s[at, :]))
            grad_weights = dot(values[spot(step), :], grads_t)
            dlogits = (weights * (grad_weights - delta)).astype(jnp.bfloat16)
            key_total[blocks(step)] += blocked(dot(dlogits, query_s[at, :]))
            query_grad_t[...] += dot(keys_t[:, spot(step)], dlogits)
            return carry

        lax.fori_loop(0, steps, back, 0)
        query_grad_s[blocks(index)] = blocked((query_grad_t[...] * scale).astype(jnp.bfloat16).T)

    own_columns = lane * wide
    out_peers = [flipped(lane, mask, GROUP_DEV) for mask in GATHER_ORDER]
    out_device = [{"ctx": base + peer, "head": head} for peer in out_peers]

    def taken(peer):
        return pl.ds(pl.multiple_of(peer * out_rows, 16), out_rows)

    sent, stores = [], []
    for h in range(heads):
        for load in loads[2 * h : 2 * h + 2]:
            load.wait()
        for copy in head_copies[h]:
            copy.wait_recv()

        def take_head(slot, _, h=h):
            source, target = source_at[slot] * per_block, to_slot(slot)
            for land, flat, turned in (
                (query_land[h], query_s, query_t),
                (grad_land[h], grad_s, grad_t),
            ):
                rows_in = [land[source + part] for part in range(per_block)]
                rows_in = jnp.concatenate(rows_in, axis=0)
                flat[target, :] = rows_in
                turned[:, target] = rows_in.T
            return 0

        lax.fori_loop(0, GROUP_BLOCKS, take_head, 0)

        def long_tile(index, _):
            tile(0, index, False)
            return 0

        def short_tile(index, _):
            tile(LONG_TOKENS, index, True)
            return 0

        lax.fori_loop(0, (SPAN_TOKENS - LONG_TOKENS) // CHUNK, short_tile, 0)
        lax.fori_loop(0, LONG_TOKENS // CHUNK, long_tile, 0)

        def put_head(place, _, h=h):
            source, target = place_at[place], to_slot(place)
            attn_place[h, target, :] = out_s[source]
            query_grad_place[h, target, :] = query_grad_s[source]
            return 0

        lax.fori_loop(0, GROUP_BLOCKS, put_head, 0)

        out_at = pl.ds(pl.multiple_of(own_columns + h * HEAD_SIZE, HEAD_SIZE), HEAD_SIZE)
        for index, (source, target) in enumerate(
            ((attn_place, attn_out), (query_grad_place, query_grad_out))
        ):
            for step, peer in enumerate(out_peers):
                copy = copy_to(
                    source.at[h, taken(peer), :],
                    target.at[:, out_at],
                    out_send.at[h, index, step],
                    out_recv.at[h, index, step],
                    out_device[step],
                )
                copy.start()
                sent.append(copy)
            keep = pltpu.make_async_copy(
                source.at[h, taken(lane), :], target.at[:, out_at], out_local.at[2 * h + index]
            )
            keep.start()
            stores.append(keep)

    def put_pair(place, _):
        source, target = place_at[place], to_slot(place)
        pair_place[0, target, :] = (key_total[source] * scale).astype(jnp.bfloat16)
        pair_place[1, target, :] = value_total[source].astype(jnp.bfloat16)
        return 0

    lax.fori_loop(0, GROUP_BLOCKS, put_pair, 0)
    swap = copy_to(pair_place.at[1 - kind], other, swap_sems.at[0], swap_sems.at[1], sibling)
    swap.start()
    swap.wait()

    def add_pair(place, _):
        at = to_slot(place)
        total = pair_place[kind, at, :].astype(jnp.float32) + other[at, :].astype(jnp.float32)
        mine[at, :] = total.astype(jnp.bfloat16)
        return 0

    lax.fori_loop(0, GROUP_BLOCKS, add_pair, 0)
    pair_at = pl.ds(pl.multiple_of(lane // sharers * HEAD_SIZE, HEAD_SIZE), HEAD_SIZE)
    pair_landing = pair_out.at[kind, lane % sharers // 2, :, pair_at]
    keep = pltpu.make_async_copy(mine.at[taken(lane), :], pair_landing, out_local.at[2 * heads])
    keep.start()
    stores.append(keep)
    for step, peer in enumerate(out_peers):
        copy = copy_to(
            mine.at[taken(peer), :],
            pair_landing,
            part_send.at[step],
            part_recv.at[step],
            out_device[step],
        )
        copy.start()
        sent.append(copy)
    for keep in stores:
        keep.wait()
    for pair in pairs:
        pair.wait_send()
    for copies in head_copies:
        for copy in copies:
            copy.wait_send()
    for copy in sent:
        copy.wait()


def fused(head_dim, query, grad, key, value, doc_blocks, block_perm):
    rows, width = query.shape
    unit = math.gcd(rows, MASK_BLOCK_SIZE)
    members = GROUP_DEV * head_dim
    wide = width // members
    heads = wide // HEAD_SIZE
    sharers = RATIO // heads
    tokens = rows * members
    out_rows = tokens // GROUP_DEV
    any_spec = pl.BlockSpec(memory_space=pl.ANY)
    smem = pl.BlockSpec(memory_space=pltpu.SMEM)

    def low(*shape):
        return pltpu.VMEM(shape, jnp.bfloat16)

    def full(*shape):
        return pltpu.VMEM(shape, jnp.float32)

    dma = pltpu.SemaphoreType.DMA
    flat, turned = (tokens, HEAD_SIZE), (HEAD_SIZE, tokens)
    landed = (tokens // unit, unit, HEAD_SIZE)
    blocked = (tokens // MASK_BLOCK_SIZE, MASK_BLOCK_SIZE, HEAD_SIZE)
    query, grad, key, value = (
        array.reshape(rows // unit, unit, -1) for array in (query, grad, key, value)
    )
    return pl.pallas_call(
        partial(fused_kernel, head_dim, heads),
        out_shape=[
            jax.ShapeDtypeStruct((out_rows, wide * GROUP_DEV), jnp.bfloat16),
            jax.ShapeDtypeStruct((out_rows, wide * GROUP_DEV), jnp.bfloat16),
            jax.ShapeDtypeStruct(
                (2, sharers // 2, out_rows, HEAD_SIZE * GROUP_DEV // sharers), jnp.bfloat16
            ),
        ],
        in_specs=[smem, smem] + [any_spec] * 4,
        out_specs=[any_spec] * 3,
        scratch_shapes=[low(*landed) for _ in range(2 * heads)]
        + [low(2, *landed)]
        + [low(*flat), low(*flat), low(*turned), low(*turned)] * 2
        + [full(LONG_TOKENS, CHUNK), full(HEAD_SIZE, CHUNK), full(HEAD_SIZE, CHUNK)]
        + [full(*blocked), full(*blocked), low(*blocked), low(*blocked)]
        + [low(heads, *flat), low(heads, *flat), low(2, *flat), low(*flat), low(*flat)]
        + [pltpu.SMEM((GROUP_BLOCKS,), jnp.int32)] * 3
        + [dma((heads, 2, members - 1))] * 2
        + [dma((members - 1,))] * 2
        + [dma((members,))] * 2
        + [dma((heads, 2, GROUP_DEV - 1))] * 2
        + [dma((GROUP_DEV - 1,))] * 2
        + [dma((2,)), dma((2 * heads + 1,)), dma((2 * heads + 1,))],
        compiler_params=pltpu.CompilerParams(
            collective_id=0, has_side_effects=True, vmem_limit_bytes=60 * 1024 * 1024
        ),
        name="fused",
    )(doc_blocks, block_perm, query, grad, key, value)


def body(head_dim, query_rows, key_rows, value_rows, grad_rows, doc_blocks, block_perm):
    attn, query_grad, parts = fused(
        head_dim, query_rows, grad_rows, key_rows, value_rows, doc_blocks, block_perm
    )
    if parts.shape[1] > 1:
        parts = jnp.sum(parts.astype(jnp.float32), axis=1).astype(jnp.bfloat16)
    else:
        parts = parts[:, 0]
    return attn, query_grad, parts[0], parts[1]


def solution(mesh):
    split = P(("ctx", "head"), None)
    out_spec = P("ctx", "head")
    return jax.shard_map(
        partial(body, mesh.shape["head"]),
        mesh=mesh,
        in_specs=(split, split, split, split, P(), P()),
        out_specs=(out_spec,) * 4,
        check_vma=False,
    )
```

time: 267 us -> 175 us (0.66)
  Pallas kernels: 252 us -> 167 us
  other arithmetic: 4.77 us -> 0 us
    pallas_call x3 -> x1, Pallas kernels: 252 us -> 167 us  [fused(): pl.pallas_call(partial(fused_kernel, head_dim, heads), out_shape=[jax.Sha...]
where the time goes in v1:
time: 175 us
  Pallas kernels  167 us (95%)
  local copies, waits for them, and re-layouts  7.77 us (4%)
    pallas_call x1, Pallas kernels, fused(): pl.pallas_call(partial(fused_kernel, head_dim, heads), out_shape=[jax.Sha...  167 us
    unnamed x4, local copies, waits for them, and re-layouts  5.72 us

profile of v1, /device:TPU:0, one launch (start us, length us, event | category | flops | bytes accessed | tf_op | source)
XLA Modules:
  0.0 175.3 jit_solution(9174749554894236542)
XLA Ops:
  0.6 166.9 %fused.1 = (bf16[384,4096]{1,0:T(8,128)(2,1)}, bf16[384,4096]{1,0:T(8,128)(2,1)}, bf16[2,1,384,512]{3,2,1,0:T(8,128)(2,1)}) custom-call(s32[2,3]{1,0:T(2,128)} %refs_0_.1, s32[48]{0:T(128)} %refs_1_.1, bf16[3,64,8192]{2,1,0:T(8,128)(2,1)} %bitcast.8, bf16[3,64,8192]{2,1,0:T(8,128)(2,1)} %bitcast.9, bf16[3,64,1024]{2,1,0:T(8,128)(2,1)} %bitcast.10, ...), custom_call_target="tpu_custom_call" | custom-call | tf_op jit(solution)/shard_map/fused/pallas_call | solution.py:483
  167.5 2.0 %slice_bitcast_fusion = (bf16[384,512]{1,0:T(8,128)(2,1)}, bf16[384,512]{1,0:T(8,128)(2,1)}) fusion(bf16[2,1,384,512]{3,2,1,0:T(8,128)(2,1)} %get-tuple-element.9), kind=kLoop, calls=%fused_computation | loop fusion | bytes 1572864 | tf_op jit(solution)/shard_map/squeeze | solution.py:522
  169.5 0.0 copy-start
  169.5 4.1 %copy.12 = bf16[384,4096]{1,0:T(8,128)(2,1)} copy(bf16[384,4096]{1,0:T(8,128)(2,1)} %get-tuple-element.16) | data formatting | bytes 6291456
  173.6 0.0 copy-done
  173.6 1.7 copy.13
Async XLA Ops:
  169.5 4.1 %copy-start = (bf16[384,4096]{1,0:T(8,128)(2,1)S(1)}, bf16[384,4096]{1,0:T(8,128)(2,1)}, u32[]{:S(2)}) copy-start(bf16[384,4096]{1,0:T(8,128)(2,1)} %get-tuple-element.17) | copy-start | bytes 9437188

commit v2 on v1

--- a/solution.py
+++ b/solution.py
@@ -23,7 +23,7 @@
 LONG_TOKENS = MOST * MASK_BLOCK_SIZE
 MESH = pl.DeviceIdType.MESH
 
-SPREAD_ORDER = [13, 5, 9, 15, 7, 11, 12, 4, 8, 14, 6, 10, 1, 3, 2]
+SPREAD_ORDER = [13, 4, 8, 15, 6, 10, 5, 12, 9, 7, 14, 11, 1, 3, 2]
 GATHER_ORDER = [6, 2, 4, 7, 3, 5, 1]
 
 
@@ -478,7 +478,11 @@
     landed = (tokens // unit, unit, HEAD_SIZE)
     blocked = (tokens // MASK_BLOCK_SIZE, MASK_BLOCK_SIZE, HEAD_SIZE)
     query, grad, key, value = (
-        array.reshape(rows // unit, unit, -1) for array in (query, grad, key, value)
+        pltpu.with_memory_space_constraint(array.reshape(rows // unit, unit, -1), pltpu.HBM)
+        for array in (query, grad, key, value)
+    )
+    doc_blocks, block_perm = (
+        pltpu.with_memory_space_constraint(array, pltpu.HBM) for array in (doc_blocks, block_perm)
     )
     return pl.pallas_call(
         partial(fused_kernel, head_dim, heads),
@@ -505,7 +509,7 @@
         + [dma((GROUP_DEV - 1,))] * 2
         + [dma((2,)), dma((2 * heads + 1,)), dma((2 * heads + 1,))],
         compiler_params=pltpu.CompilerParams(
-            collective_id=0, has_side_effects=True, vmem_limit_bytes=60 * 1024 * 1024
+            collective_id=0, has_side_effects=True, vmem_limit_bytes=40 * 1024 * 1024
         ),
         name="fused",
     )(doc_blocks, block_perm, query, grad, key, value)

time: 175 us -> 169 us (0.966)
  local copies, waits for them, and re-layouts: 7.77 us -> 4.25 us
  Pallas kernels: 167 us -> 164 us
    pallas_call x1, Pallas kernels: 167 us -> 164 us  [fused(): pl.pallas_call(partial(fused_kernel, head_dim, heads), out_shape=[jax.Sha...]
    unnamed x4 -> x2, local copies, waits for them, and re-layouts: 5.72 us -> 3.33 us
where the time goes in v2:
time: 169 us
  Pallas kernels  164 us (97%)
  local copies, waits for them, and re-layouts  4.25 us (3%)
    pallas_call x1, Pallas kernels, fused(): pl.pallas_call(partial(fused_kernel, head_dim, heads), out_shape=[jax.Sha...  164 us

profile of v2, /device:TPU:0, one launch (start us, length us, event | category | flops | bytes accessed | tf_op | source)
XLA Modules:
  0.0 169.1 jit_solution(3910056936814987846)
XLA Ops:
  0.6 164.3 %fused.1 = (bf16[384,4096]{1,0:T(8,128)(2,1)S(1)}, bf16[384,4096]{1,0:T(8,128)(2,1)S(1)}, bf16[2,1,384,512]{3,2,1,0:T(8,128)(2,1)S(1)}) custom-call(s32[2,3]{1,0:T(2,128)} %refs_0_.1, s32[48]{0:T(128)} %refs_1_.1, bf16[3,64,8192]{2,1,0:T(8,128)(2,1)} %bitcast.8, bf16[3,64,8192]{2,1,0:T(8,128)(2,1)} %bitcast.9, bf16[3,64,1024]{2,1,0:T(8,128)(2,1)} %bitcast.10, ...), custom_call_target="tpu_custom_call" | custom-call | tf_op jit(solution)/shard_map/fused/pallas_call | solution.py:487
  164.9 0.9 slice_bitcast_fusion
  165.8 1.7 copy.12
  167.5 1.7 copy.13

commit v3 on v2

--- a/solution.py
+++ b/solution.py
@@ -21,10 +21,14 @@
 CHUNK = 512
 SPAN_TOKENS = GROUP_BLOCKS * MASK_BLOCK_SIZE
 LONG_TOKENS = MOST * MASK_BLOCK_SIZE
+PIECES = 2
 MESH = pl.DeviceIdType.MESH
 
-SPREAD_ORDER = [13, 4, 8, 15, 6, 10, 5, 12, 9, 7, 14, 11, 1, 3, 2]
-GATHER_ORDER = [6, 2, 4, 7, 3, 5, 1]
+SPREAD_ORDERS = [
+    [13, 4, 8, 15, 6, 10, 5, 12, 9, 7, 14, 11, 1, 3, 2],
+    [13, 4, 8, 15, 6, 10, 5, 12, 9, 7, 14, 11, 1, 3, 2],
+]
+GATHER_ORDERS = [[6, 4, 2, 7, 5, 3, 1], [2, 5, 6, 3, 4, 7, 1]]
 
 
 def enter(peers):
@@ -43,8 +47,9 @@
     return result
 
 
-def visiting_order(members):
-    return SPREAD_ORDER if len(SPREAD_ORDER) == members - 1 else list(range(members - 1, 0, -1))
+def visiting_order(kind, members):
+    order = SPREAD_ORDERS[kind]
+    return order if len(order) == members - 1 else list(range(members - 1, 0, -1))
 
 
 def dot(left, right):
@@ -98,7 +103,6 @@
     lane = ctx - base
     kind = lane % 2
     own = lane * head_dim + head
-    order = visiting_order(members)
 
     def rows_of(member):
         return pl.ds(member * units, units)
@@ -114,9 +118,9 @@
         )
 
     landing = rows_of(own)
-    masks = [(mask, flipped(own, mask, members)) for mask in order]
-    peers = [(mask, member, member // head_dim, member % head_dim) for mask, member in masks]
-    device = [{"ctx": base + peer_lane, "head": peer_head} for _, _, peer_lane, peer_head in peers]
+    members_at = [flipped(own, mask, members) for mask in range(members)]
+    peers = [(member // head_dim, member % head_dim) for member in members_at]
+    device = [{"ctx": base + peer_lane, "head": peer_head} for peer_lane, peer_head in peers]
     sibling = {"ctx": base + flipped(lane, 1, GROUP_DEV), "head": head}
 
     def own_pair(own_kind):
@@ -126,14 +130,23 @@
             local_sems.at[2 * heads],
         )
 
-    def pair_copy(step, peer_kind):
-        _, _, peer_lane, peer_head = peers[step]
+    def pair_copy(mask, peer_kind):
         return copy_to(
-            (key_ref, value_ref)[peer_kind].at[:, :, key_columns(peer_lane, peer_head)],
+            (key_ref, value_ref)[peer_kind].at[:, :, key_columns(*peers[mask])],
             pair_land.at[peer_kind, landing],
-            pair_send.at[step],
-            pair_recv.at[step],
-            device[step],
+            pair_send.at[mask - 1],
+            pair_recv.at[mask - 1],
+            device[mask],
+        )
+
+    def head_copy(h, index, mask):
+        source, target = ((query_ref, query_land[h]), (grad_ref, grad_land[h]))[index]
+        return copy_to(
+            source.at[:, :, head_columns(*peers[mask], h)],
+            target.at[landing],
+            in_send.at[h, index, mask - 1],
+            in_recv.at[h, index, mask - 1],
+            device[mask],
         )
 
     loads = []
@@ -153,32 +166,18 @@
         def _(own_kind=own_kind):
             own_pair(own_kind).start()
 
-    enter(device)
+    enter(device[1:])
     for own_kind in range(2):
 
         @pl.when(kind == own_kind)
         def _(own_kind=own_kind):
-            for step, (mask, _, _, _) in enumerate(peers):
-                pair_copy(step, (own_kind + mask // head_dim) % 2).start()
-
-    head_copies = []
-    for h in range(heads):
-        copies = []
-        for step, (_, _, peer_lane, peer_head) in enumerate(peers):
-            at = head_columns(peer_lane, peer_head, h)
-            for index, (source, target) in enumerate(
-                ((query_ref, query_land[h]), (grad_ref, grad_land[h]))
-            ):
-                copy = copy_to(
-                    source.at[:, :, at],
-                    target.at[landing],
-                    in_send.at[h, index, step],
-                    in_recv.at[h, index, step],
-                    device[step],
-                )
-                copy.start()
-                copies.append(copy)
-        head_copies.append(copies)
+            order = visiting_order(own_kind, members)
+            for mask in order:
+                pair_copy(mask, (own_kind + mask // head_dim) % 2).start()
+            for h in range(heads):
+                for mask in order:
+                    for index in range(2):
+                        head_copy(h, index, mask).start()
 
     lengths = [docs_ref[group, i] for i in range(docs_ref.shape[1])]
     starts, start = [], jnp.int32(0)
@@ -241,17 +240,18 @@
     ).wait()
     passes = [passing(members - 1, landing)]
     pairs = []
-    for step, (_, member, _, _) in enumerate(peers):
+    for mask in visiting_order(0, members):
+        spot = rows_of(members_at[mask])
         pair = copy_to(
             key_ref.at[:, :, key_columns(lane, head)],
-            pair_land.at[kind, rows_of(member)],
-            pair_send.at[step],
-            pair_recv.at[step],
-            device[step],
+            pair_land.at[kind, spot],
+            pair_send.at[mask - 1],
+            pair_recv.at[mask - 1],
+            device[mask],
         )
         pair.wait_recv()
         pairs.append(pair)
-        passes.append(passing(step, rows_of(member)))
+        passes.append(passing(mask - 1, spot))
     for copy in passes:
         copy.wait()
 
@@ -345,18 +345,20 @@
         query_grad_s[blocks(index)] = blocked((query_grad_t[...] * scale).astype(jnp.bfloat16).T)
 
     own_columns = lane * wide
-    out_peers = [flipped(lane, mask, GROUP_DEV) for mask in GATHER_ORDER]
+    out_peers = [flipped(lane, mask, GROUP_DEV) for mask in range(GROUP_DEV)]
     out_device = [{"ctx": base + peer, "head": head} for peer in out_peers]
 
     def taken(peer):
         return pl.ds(pl.multiple_of(peer * out_rows, 16), out_rows)
 
-    sent, stores = [], []
+    received, sent, stores = [], [], []
     for h in range(heads):
         for load in loads[2 * h : 2 * h + 2]:
             load.wait()
-        for copy in head_copies[h]:
+        copies = [head_copy(h, i, mask) for mask in range(1, members) for i in range(2)]
+        for copy in copies:
             copy.wait_recv()
+        received.extend(copies)
 
         def take_head(slot, _, h=h):
             source, target = source_at[slot] * per_block, to_slot(slot)
@@ -392,19 +394,29 @@
         lax.fori_loop(0, GROUP_BLOCKS, put_head, 0)
 
         out_at = pl.ds(pl.multiple_of(own_columns + h * HEAD_SIZE, HEAD_SIZE), HEAD_SIZE)
+
+        def out_copy(index, mask, h=h, out_at=out_at):
+            source, target = ((attn_place, attn_out), (query_grad_place, query_grad_out))[index]
+            return copy_to(
+                source.at[h, taken(out_peers[mask]), :],
+                target.at[:, out_at],
+                out_send.at[h, index, mask - 1],
+                out_recv.at[h, index, mask - 1],
+                out_device[mask],
+            )
+
+        for own_kind in range(2):
+
+            @pl.when(kind == own_kind)
+            def _(own_kind=own_kind, out_copy=out_copy):
+                for index in range(2):
+                    for mask in GATHER_ORDERS[own_kind]:
+                        out_copy(index, mask).start()
+
+        sent.extend(out_copy(i, mask) for i in range(2) for mask in range(1, GROUP_DEV))
         for index, (source, target) in enumerate(
             ((attn_place, attn_out), (query_grad_place, query_grad_out))
         ):
-            for step, peer in enumerate(out_peers):
-                copy = copy_to(
-                    source.at[h, taken(peer), :],
-                    target.at[:, out_at],
-                    out_send.at[h, index, step],
-                    out_recv.at[h, index, step],
-                    out_device[step],
-                )
-                copy.start()
-                sent.append(copy)
             keep = pltpu.make_async_copy(
                 source.at[h, taken(lane), :], target.at[:, out_at], out_local.at[2 * h + index]
             )
@@ -434,13 +446,13 @@
     keep = pltpu.make_async_copy(mine.at[taken(lane), :], pair_landing, out_local.at[2 * heads])
     keep.start()
     stores.append(keep)
-    for step, peer in enumerate(out_peers):
+    for mask in GATHER_ORDERS[0]:
         copy = copy_to(
-            mine.at[taken(peer), :],
+            mine.at[taken(out_peers[mask]), :],
             pair_landing,
-            part_send.at[step],
-            part_recv.at[step],
-            out_device[step],
+            part_send.at[mask - 1],
+            part_recv.at[mask - 1],
+            out_device[mask],
         )
         copy.start()
         sent.append(copy)
@@ -448,9 +460,8 @@
         keep.wait()
     for pair in pairs:
         pair.wait_send()
-    for copies in head_copies:
-        for copy in copies:
-            copy.wait_send()
+    for copy in received:
+        copy.wait_send()
     for copy in sent:
         copy.wait()
 
@@ -515,14 +526,48 @@
     )(doc_blocks, block_perm, query, grad, key, value)
 
 
+def keep_kernel(attn_ref, query_ref, parts_ref, attn_out, query_out, key_out, value_out, sems):
+    rows = attn_ref.shape[0] // PIECES
+    copies = []
+    for piece in range(PIECES):
+        at = pl.ds(piece * rows, rows)
+        for index, (source, target) in enumerate(
+            (
+                (attn_ref.at[at, :], attn_out.at[at, :]),
+                (query_ref.at[at, :], query_out.at[at, :]),
+                (parts_ref.at[0, 0, at, :], key_out.at[at, :]),
+                (parts_ref.at[1, 0, at, :], value_out.at[at, :]),
+            )
+        ):
+            copies.append(pltpu.make_async_copy(source, target, sems.at[index, piece]))
+    for copy in copies:
+        copy.start()
+    for copy in copies:
+        copy.wait()
+
+
+def keep(attn, query_grad, parts):
+    any_spec = pl.BlockSpec(memory_space=pl.ANY)
+    part = jax.ShapeDtypeStruct(parts.shape[2:], jnp.bfloat16)
+    whole = jax.ShapeDtypeStruct(attn.shape, jnp.bfloat16)
+    return pl.pallas_call(
+        keep_kernel,
+        out_shape=[whole, whole, part, part],
+        in_specs=[any_spec] * 3,
+        out_specs=[any_spec] * 4,
+        scratch_shapes=[pltpu.SemaphoreType.DMA((4, PIECES))],
+        compiler_params=pltpu.CompilerParams(vmem_limit_bytes=1024 * 1024),
+        name="keep",
+    )(attn, query_grad, parts)
+
+
 def body(head_dim, query_rows, key_rows, value_rows, grad_rows, doc_blocks, block_perm):
     attn, query_grad, parts = fused(
         head_dim, query_rows, grad_rows, key_rows, value_rows, doc_blocks, block_perm
     )
-    if parts.shape[1] > 1:
-        parts = jnp.sum(parts.astype(jnp.float32), axis=1).astype(jnp.bfloat16)
-    else:
-        parts = parts[:, 0]
+    if parts.shape[1] == 1:
+        return keep(attn, query_grad, parts)
+    parts = jnp.sum(parts.astype(jnp.float32), axis=1).astype(jnp.bfloat16)
     return attn, query_grad, parts[0], parts[1]
 
 

time: 169 us -> 168 us (level)
  local copies, waits for them, and re-layouts: 4.25 us -> 0 us
  Pallas kernels: 164 us -> 167 us
    unnamed x2 -> x0, local copies, waits for them, and re-layouts: 3.33 us -> none
    pallas_call x0 -> x1, Pallas kernels: none -> 2.96 us  [keep(): pl.pallas_call(keep_kernel, out_shape=[whole, whole, part, part], in_spec...]
where the time goes in v3:
time: 168 us
  Pallas kernels  167 us (99%)
    pallas_call x1, Pallas kernels, fused(): pl.pallas_call(partial(fused_kernel, head_dim, heads), out_shape=[jax.Sha...  164 us

profile of v3, /device:TPU:0, one launch (start us, length us, event | category | flops | bytes accessed | tf_op | source)
XLA Modules:
  0.0 168.0 jit_solution(6078077928379250181)
XLA Ops:
  0.6 164.2 %fused.1 = (bf16[384,4096]{1,0:T(8,128)(2,1)S(1)}, bf16[384,4096]{1,0:T(8,128)(2,1)S(1)}, bf16[2,1,384,512]{3,2,1,0:T(8,128)(2,1)S(1)}) custom-call(s32[2,3]{1,0:T(2,128)} %refs_0_.1, s32[48]{0:T(128)} %refs_1_.1, bf16[3,64,8192]{2,1,0:T(8,128)(2,1)} %bitcast.4, bf16[3,64,8192]{2,1,0:T(8,128)(2,1)} %bitcast.5, bf16[3,64,1024]{2,1,0:T(8,128)(2,1)} %bitcast.6, ...), custom_call_target="tpu_custom_call" | custom-call | tf_op jit(solution)/shard_map/fused/pallas_call | solution.py:498
  164.8 3.0 %keep.1 = (bf16[384,4096]{1,0:T(8,128)(2,1)}, bf16[384,4096]{1,0:T(8,128)(2,1)}, bf16[384,512]{1,0:T(8,128)(2,1)}, bf16[384,512]{1,0:T(8,128)(2,1)}) custom-call(bf16[384,4096]{1,0:T(8,128)(2,1)S(1)} %get-tuple-element.7.attn_ref, bf16[384,4096]{1,0:T(8,128)(2,1)S(1)} %get-tuple-element.8.query_ref, bf16[2,1,384,512]{3,2,1,0:T(8,128)(2,1)S(1)} %get-tuple-element.9.parts_ref), custom_call_target="tpu_custom_call" | custom-call | tf_op jit(solution)/shard_map/keep/pallas_call | solution.py:553

commit v4 on v3

--- a/solution.py
+++ b/solution.py
@@ -21,6 +21,8 @@
 CHUNK = 512
 SPAN_TOKENS = GROUP_BLOCKS * MASK_BLOCK_SIZE
 LONG_TOKENS = MOST * MASK_BLOCK_SIZE
+IN_GROUPS = ((0, 1), (1, 1), (2, 2))
+OUT_GROUPS = ((0, 2), (2, 1), (3, 1))
 PIECES = 2
 MESH = pl.DeviceIdType.MESH
 
@@ -31,11 +33,10 @@
 GATHER_ORDERS = [[6, 4, 2, 7, 5, 3, 1], [2, 5, 6, 3, 4, 7, 1]]
 
 
-def enter(peers):
+def greet(peers):
     barrier = pltpu.get_barrier_semaphore()
     for peer in peers:
         pl.semaphore_signal(barrier, inc=1, device_id=peer, device_id_type=MESH)
-    pl.semaphore_wait(barrier, len(peers))
 
 
 def flipped(index, mask, count):
@@ -50,6 +51,12 @@
 def visiting_order(kind, members):
     order = SPREAD_ORDERS[kind]
     return order if len(order) == members - 1 else list(range(members - 1, 0, -1))
+
+
+def grouped(groups, heads):
+    if sum(count for _, count in groups) == heads:
+        return groups
+    return tuple((h, 1) for h in range(heads))
 
 
 def dot(left, right):
@@ -76,11 +83,13 @@
 
     docs_ref, perm_ref, query_ref, grad_ref, key_ref, value_ref = take(6)
     attn_out, query_grad_out, pair_out = take(3)
-    query_land, grad_land = take(heads), take(heads)
+    in_groups, out_groups = grouped(IN_GROUPS, heads), grouped(OUT_GROUPS, heads)
+    query_land, grad_land = take(len(in_groups)), take(len(in_groups))
     (pair_land,) = take(1)
     query_s, grad_s, query_t, grad_t, keys, values, keys_t, values_t = take(8)
     store, out_t, query_grad_t, key_total, value_total, out_s, query_grad_s = take(7)
-    attn_place, query_grad_place, pair_place, other, mine = take(5)
+    attn_place, query_grad_place = take(len(out_groups)), take(len(out_groups))
+    pair_place, other, mine = take(3)
     slot_at, source_at, place_at = take(3)
     in_send, in_recv, pair_send, pair_recv, pass_send, pass_recv = take(6)
     out_send, out_recv, part_send, part_recv, swap_sems, local_sems, out_local = take(7)
@@ -107,9 +116,10 @@
     def rows_of(member):
         return pl.ds(member * units, units)
 
-    def head_columns(peer_lane, peer_head, h):
-        worker = peer_head * GROUP_DEV + peer_lane
-        return pl.ds(pl.multiple_of(worker * wide + h * HEAD_SIZE, HEAD_SIZE), HEAD_SIZE)
+    def head_columns(peer_lane, peer_head, g):
+        first, count = in_groups[g]
+        start = (peer_head * GROUP_DEV + peer_lane) * wide + first * HEAD_SIZE
+        return pl.ds(pl.multiple_of(start, HEAD_SIZE), count * HEAD_SIZE)
 
     def key_columns(peer_lane, peer_head):
         worker = peer_head * GROUP_DEV + peer_lane
@@ -149,8 +159,9 @@
             device[mask],
         )
 
+    greet(device[1:])
     loads = []
-    for h in range(heads):
+    for h in range(len(in_groups)):
         at = head_columns(lane, head, h)
         for index, (source, target) in enumerate(
             ((query_ref, query_land[h]), (grad_ref, grad_land[h]))
@@ -166,7 +177,7 @@
         def _(own_kind=own_kind):
             own_pair(own_kind).start()
 
-    enter(device[1:])
+    pl.semaphore_wait(pltpu.get_barrier_semaphore(), members - 1)
     for own_kind in range(2):
 
         @pl.when(kind == own_kind)
@@ -174,9 +185,9 @@
             order = visiting_order(own_kind, members)
             for mask in order:
                 pair_copy(mask, (own_kind + mask // head_dim) % 2).start()
-            for h in range(heads):
-                for mask in order:
-                    for index in range(2):
+            for h in range(len(in_groups)):
+                for index in range(2):
+                    for mask in order:
                         head_copy(h, index, mask).start()
 
     lengths = [docs_ref[group, i] for i in range(docs_ref.shape[1])]
@@ -353,20 +364,23 @@
 
     received, sent, stores = [], [], []
     for h in range(heads):
-        for load in loads[2 * h : 2 * h + 2]:
-            load.wait()
-        copies = [head_copy(h, i, mask) for mask in range(1, members) for i in range(2)]
-        for copy in copies:
-            copy.wait_recv()
-        received.extend(copies)
-
-        def take_head(slot, _, h=h):
+        g, column = [(g, h - first) for g, (first, n) in enumerate(in_groups) if first <= h < first + n][0]
+        column = slice(column * HEAD_SIZE, (column + 1) * HEAD_SIZE)
+        if column.start == 0:
+            for load in loads[2 * g : 2 * g + 2]:
+                load.wait()
+            copies = [head_copy(g, i, mask) for mask in range(1, members) for i in range(2)]
+            for copy in copies:
+                copy.wait_recv()
+            received.extend(copies)
+
+        def take_head(slot, _, g=g, column=column):
             source, target = source_at[slot] * per_block, to_slot(slot)
             for land, flat, turned in (
-                (query_land[h], query_s, query_t),
-                (grad_land[h], grad_s, grad_t),
+                (query_land[g], query_s, query_t),
+                (grad_land[g], grad_s, grad_t),
             ):
-                rows_in = [land[source + part] for part in range(per_block)]
+                rows_in = [land[source + part][:, column] for part in range(per_block)]
                 rows_in = jnp.concatenate(rows_in, axis=0)
                 flat[target, :] = rows_in
                 turned[:, target] = rows_in.T
@@ -385,23 +399,30 @@
         lax.fori_loop(0, (SPAN_TOKENS - LONG_TOKENS) // CHUNK, short_tile, 0)
         lax.fori_loop(0, LONG_TOKENS // CHUNK, long_tile, 0)
 
-        def put_head(place, _, h=h):
+        o, out_column = [(g, h - first) for g, (first, n) in enumerate(out_groups) if first <= h < first + n][0]
+        first, count = out_groups[o]
+        column = slice(out_column * HEAD_SIZE, (out_column + 1) * HEAD_SIZE)
+
+        def put_head(place, _, o=o, column=column):
             source, target = place_at[place], to_slot(place)
-            attn_place[h, target, :] = out_s[source]
-            query_grad_place[h, target, :] = query_grad_s[source]
+            attn_place[o][target, column] = out_s[source]
+            query_grad_place[o][target, column] = query_grad_s[source]
             return 0
 
         lax.fori_loop(0, GROUP_BLOCKS, put_head, 0)
 
-        out_at = pl.ds(pl.multiple_of(own_columns + h * HEAD_SIZE, HEAD_SIZE), HEAD_SIZE)
-
-        def out_copy(index, mask, h=h, out_at=out_at):
+        if h + 1 < first + count:
+            continue
+        out_at = own_columns + first * HEAD_SIZE
+        out_at = pl.ds(pl.multiple_of(out_at, HEAD_SIZE), count * HEAD_SIZE)
+
+        def out_copy(index, mask, o=o, out_at=out_at):
             source, target = ((attn_place, attn_out), (query_grad_place, query_grad_out))[index]
             return copy_to(
-                source.at[h, taken(out_peers[mask]), :],
+                source[o].at[taken(out_peers[mask]), :],
                 target.at[:, out_at],
-                out_send.at[h, index, mask - 1],
-                out_recv.at[h, index, mask - 1],
+                out_send.at[o, index, mask - 1],
+                out_recv.at[o, index, mask - 1],
                 out_device[mask],
             )
 
@@ -418,7 +439,7 @@
             ((attn_place, attn_out), (query_grad_place, query_grad_out))
         ):
             keep = pltpu.make_async_copy(
-                source.at[h, taken(lane), :], target.at[:, out_at], out_local.at[2 * h + index]
+                source[o].at[taken(lane), :], target.at[:, out_at], out_local.at[2 * o + index]
             )
             keep.start()
             stores.append(keep)
@@ -485,6 +506,7 @@
         return pltpu.VMEM(shape, jnp.float32)
 
     dma = pltpu.SemaphoreType.DMA
+    in_groups, out_groups = grouped(IN_GROUPS, heads), grouped(OUT_GROUPS, heads)
     flat, turned = (tokens, HEAD_SIZE), (HEAD_SIZE, tokens)
     landed = (tokens // unit, unit, HEAD_SIZE)
     blocked = (tokens // MASK_BLOCK_SIZE, MASK_BLOCK_SIZE, HEAD_SIZE)
@@ -506,12 +528,13 @@
         ],
         in_specs=[smem, smem] + [any_spec] * 4,
         out_specs=[any_spec] * 3,
-        scratch_shapes=[low(*landed) for _ in range(2 * heads)]
+        scratch_shapes=[low(*landed[:2], n * HEAD_SIZE) for _, n in in_groups * 2]
         + [low(2, *landed)]
         + [low(*flat), low(*flat), low(*turned), low(*turned)] * 2
         + [full(LONG_TOKENS, CHUNK), full(HEAD_SIZE, CHUNK), full(HEAD_SIZE, CHUNK)]
         + [full(*blocked), full(*blocked), low(*blocked), low(*blocked)]
-        + [low(heads, *flat), low(heads, *flat), low(2, *flat), low(*flat), low(*flat)]
+        + [low(tokens, n * HEAD_SIZE) for _, n in out_groups * 2]
+        + [low(2, *flat), low(*flat), low(*flat)]
         + [pltpu.SMEM((GROUP_BLOCKS,), jnp.int32)] * 3
         + [dma((heads, 2, members - 1))] * 2
         + [dma((members - 1,))] * 2

time: 168 us -> 167 us (level)
  no operation moved by 1% of the time
where the time goes in v4:
time: 167 us
  Pallas kernels  167 us (100%)
    pallas_call x1, Pallas kernels, fused(): pl.pallas_call(partial(fused_kernel, head_dim, heads), out_shape=[jax.Sha...  164 us

profile of v4, /device:TPU:0, one launch (start us, length us, event | category | flops | bytes accessed | tf_op | source)
XLA Modules:
  0.0 167.3 jit_solution(9013737516101971983)
XLA Ops:
  0.6 163.5 %fused.1 = (bf16[384,4096]{1,0:T(8,128)(2,1)S(1)}, bf16[384,4096]{1,0:T(8,128)(2,1)S(1)}, bf16[2,1,384,512]{3,2,1,0:T(8,128)(2,1)S(1)}) custom-call(s32[2,3]{1,0:T(2,128)} %refs_0_.1, s32[48]{0:T(128)} %refs_1_.1, bf16[3,64,8192]{2,1,0:T(8,128)(2,1)} %bitcast.4, bf16[3,64,8192]{2,1,0:T(8,128)(2,1)} %bitcast.5, bf16[3,64,1024]{2,1,0:T(8,128)(2,1)} %bitcast.6, ...), custom_call_target="tpu_custom_call" | custom-call | tf_op jit(solution)/shard_map/fused/pallas_call | solution.py:520
  164.2 3.0 %keep.1 = (bf16[384,4096]{1,0:T(8,128)(2,1)}, bf16[384,4096]{1,0:T(8,128)(2,1)}, bf16[384,512]{1,0:T(8,128)(2,1)}, bf16[384,512]{1,0:T(8,128)(2,1)}) custom-call(bf16[384,4096]{1,0:T(8,128)(2,1)S(1)} %get-tuple-element.7.attn_ref, bf16[384,4096]{1,0:T(8,128)(2,1)S(1)} %get-tuple-element.8.query_ref, bf16[2,1,384,512]{3,2,1,0:T(8,128)(2,1)S(1)} %get-tuple-element.9.parts_ref), custom_call_target="tpu_custom_call" | custom-call | tf_op jit(solution)/shard_map/keep/pallas_call | solution.py:576

commit v5 on v4

--- a/solution.py
+++ b/solution.py
@@ -285,19 +285,25 @@
 
     def tile(first, index, short):
         at = pl.ds(pl.multiple_of(first + index * CHUNK, CHUNK), CHUNK)
-        steps = index + 1
-
-        def spot(step):
-            return pl.ds(pl.multiple_of(first + step * CHUNK, CHUNK), CHUNK)
-
-        def slot(step):
-            return pl.ds(pl.multiple_of(step * CHUNK, CHUNK), CHUNK)
+        half = CHUNK // 2
+
+        def part(step, low, size):
+            start = step * CHUNK + low
+            spot = pl.ds(pl.multiple_of(first + start, half), size)
+            slot = pl.ds(pl.multiple_of(start, half), size)
+            return spot, slot, pl.ds((first + start) // block, size // block)
 
         def blocks(step):
             return pl.ds(first // block + step * per_chunk, per_chunk)
 
         def blocked(array):
-            return array.reshape(per_chunk, block, HEAD_SIZE)
+            return array.reshape(array.shape[0] // block, block, HEAD_SIZE)
+
+        corner = pl.ds(pl.multiple_of(first + index * CHUNK + half, half), half)
+        pieces = ((0, half, at, slice(0, CHUNK)), (half, half, corner, slice(half, CHUNK)))
+
+        def joined(left, right):
+            return jnp.concatenate([left[:, :half], right], axis=1)
 
         queries_t = query_t[:, at]
         grads_t = grad_t[:, at]
@@ -307,34 +313,46 @@
             for start in other_starts:
                 opened = jnp.maximum(opened, jnp.where(column >= start, start, 0))
 
-        def logits(step, peak, diagonal):
-            raw = dot(keys[spot(step), :], queries_t)
+        def logits(step, peak, low, size, columns, diagonal):
+            spot, slot, _ = part(step, low, size)
+            raw = dot(keys[spot, :], queries_t[:, columns])
+            keys_at = key_at[:size, columns] + low
             if diagonal:
-                allowed = key_at <= token
+                allowed = keys_at <= token[:size, columns]
                 if short:
-                    allowed = allowed & (key_at >= opened - step * CHUNK)
+                    allowed = allowed & (keys_at >= opened[:, columns] - step * CHUNK)
                 raw = jnp.where(allowed, raw, MASKED_LOGIT)
             elif short:
-                raw = jnp.where(key_at >= opened - step * CHUNK, raw, MASKED_LOGIT)
-            store[slot(step), :] = raw
-            return jnp.maximum(peak, jnp.max(raw, axis=0, keepdims=True))
-
+                raw = jnp.where(keys_at >= opened - step * CHUNK, raw, MASKED_LOGIT)
+            store[slot, columns] = raw
+            return jnp.maximum(peak[:, columns], jnp.max(raw, axis=0, keepdims=True))
+
+        everything = slice(0, CHUNK)
         peak = lax.fori_loop(
             0,
             index,
-            lambda step, peak: logits(step, peak, False),
+            lambda step, peak: logits(step, peak, 0, CHUNK, everything, False),
             jnp.full((1, CHUNK), MASKED_LOGIT, jnp.float32),
         )
-        peak = logits(index, peak, True) * scale_log2
+        peak = logits(index, peak, 0, half, everything, True)
+        peak = joined(peak, logits(index, peak, half, half, slice(half, CHUNK), True)) * scale_log2
         out_t[...] = jnp.zeros_like(out_t)
 
-        def mix(step, total):
-            mass = jnp.exp2(store[slot(step), :] * scale_log2 - peak)
-            store[slot(step), :] = mass
-            out_t[...] += dot(values_t[:, spot(step)], mass.astype(jnp.bfloat16))
-            return total + jnp.sum(mass, axis=0, keepdims=True)
-
-        total = lax.fori_loop(0, steps, mix, jnp.zeros((1, CHUNK), jnp.float32))
+        def mix(step, total, low, size, columns):
+            spot, slot, _ = part(step, low, size)
+            mass = jnp.exp2(store[slot, columns] * scale_log2 - peak[:, columns])
+            store[slot, columns] = mass
+            out_t[:, columns] += dot(values_t[:, spot], mass.astype(jnp.bfloat16))
+            return total[:, columns] + jnp.sum(mass, axis=0, keepdims=True)
+
+        total = lax.fori_loop(
+            0,
+            index,
+            lambda step, total: mix(step, total, 0, CHUNK, everything),
+            jnp.zeros((1, CHUNK), jnp.float32),
+        )
+        total = mix(index, total, 0, half, everything)
+        total = joined(total, mix(index, total, half, half, slice(half, CHUNK)))
         share = 1.0 / total
         out = (out_t[...] * share).astype(jnp.bfloat16)
         delta = jnp.sum(
@@ -343,16 +361,22 @@
         out_s[blocks(index)] = blocked(out.T)
         query_grad_t[...] = jnp.zeros_like(query_grad_t)
 
-        def back(step, carry):
-            weights = store[slot(step), :] * share
-            value_total[blocks(step)] += blocked(dot(weights.astype(jnp.bfloat16), grad_s[at, :]))
-            grad_weights = dot(values[spot(step), :], grads_t)
-            dlogits = (weights * (grad_weights - delta)).astype(jnp.bfloat16)
-            key_total[blocks(step)] += blocked(dot(dlogits, query_s[at, :]))
-            query_grad_t[...] += dot(keys_t[:, spot(step)], dlogits)
+        def back(step, low, size, rows_at, columns):
+            spot, slot, spot_blocks = part(step, low, size)
+            weights = store[slot, columns] * share[:, columns]
+            value_total[spot_blocks] += blocked(dot(weights.astype(jnp.bfloat16), grad_s[rows_at, :]))
+            grad_weights = dot(values[spot, :], grads_t[:, columns])
+            dlogits = (weights * (grad_weights - delta[:, columns])).astype(jnp.bfloat16)
+            key_total[spot_blocks] += blocked(dot(dlogits, query_s[rows_at, :]))
+            query_grad_t[:, columns] += dot(keys_t[:, spot], dlogits)
+
+        def back_step(step, carry):
+            back(step, 0, CHUNK, at, everything)
             return carry
 
-        lax.fori_loop(0, steps, back, 0)
+        lax.fori_loop(0, index, back_step, 0)
+        for low, size, rows_at, columns in pieces:
+            back(index, low, size, rows_at, columns)
         query_grad_s[blocks(index)] = blocked((query_grad_t[...] * scale).astype(jnp.bfloat16).T)
 
     own_columns = lane * wide

time: 167 us -> 167 us (level)
  no operation moved by 1% of the time
where the time goes in v5:
time: 167 us
  Pallas kernels  167 us (100%)
    pallas_call x1, Pallas kernels, fused(): pl.pallas_call(partial(fused_kernel, head_dim, heads), out_shape=[jax.Sha...  164 us

profile of v5, /device:TPU:0, one launch (start us, length us, event | category | flops | bytes accessed | tf_op | source)
XLA Modules:
  0.0 167.3 jit_solution(14986416505165258517)
XLA Ops:
  0.6 163.5 %fused.1 = (bf16[384,4096]{1,0:T(8,128)(2,1)S(1)}, bf16[384,4096]{1,0:T(8,128)(2,1)S(1)}, bf16[2,1,384,512]{3,2,1,0:T(8,128)(2,1)S(1)}) custom-call(s32[2,3]{1,0:T(2,128)} %refs_0_.1, s32[48]{0:T(128)} %refs_1_.1, bf16[3,64,8192]{2,1,0:T(8,128)(2,1)} %bitcast.4, bf16[3,64,8192]{2,1,0:T(8,128)(2,1)} %bitcast.5, bf16[3,64,1024]{2,1,0:T(8,128)(2,1)} %bitcast.6, ...), custom_call_target="tpu_custom_call" | custom-call | tf_op jit(solution)/shard_map/fused/pallas_call | solution.py:544
  164.2 3.0 %keep.1 = (bf16[384,4096]{1,0:T(8,128)(2,1)}, bf16[384,4096]{1,0:T(8,128)(2,1)}, bf16[384,512]{1,0:T(8,128)(2,1)}, bf16[384,512]{1,0:T(8,128)(2,1)}) custom-call(bf16[384,4096]{1,0:T(8,128)(2,1)S(1)} %get-tuple-element.7.attn_ref, bf16[384,4096]{1,0:T(8,128)(2,1)S(1)} %get-tuple-element.8.query_ref, bf16[2,1,384,512]{3,2,1,0:T(8,128)(2,1)S(1)} %get-tuple-element.9.parts_ref), custom_call_target="tpu_custom_call" | custom-call | tf_op jit(solution)/shard_map/keep/pallas_call | solution.py:600
